TPU v7x, 32 devices: a whole 2x2x4 slice. The times are simulated.
32 devices in a mesh: dp: 16 (over z, y, core), query: 2 (over x).
Axes of the slice: x: 2, y: 2, z: 4, core: 2. Of those that a mesh axis runs over, the one named last changes fastest.
Arguments:
- tokens: bfloat16 [2, 32, 128, 1280], P(None, ('dp', 'query')), may hold values from -6 to 6
- out_cotangent: bfloat16 [2, 32, 128, 1280], P(None, ('dp', 'query')), may hold values from -6 to 6
- qkv_weight: bfloat16 [1280, 3840], P('dp'), may hold values from -0.15625 to 0.15625
- out_weight: bfloat16 [1280, 1280], P('dp'), may hold values from -0.625 to 0.625
- up_weight: bfloat16 [1280, 5120], P('dp'), may hold values from -0.15625 to 0.15625
- down_weight: bfloat16 [5120, 1280], P('dp'), may hold values from -0.078125 to 0.078125
- attn_gain: bfloat16 [1280], P('dp'), may hold values from 0.5 to 1.5
- ffn_gain: bfloat16 [1280], P('dp'), may hold values from 0.5 to 1.5
- up_bias: bfloat16 [5120], P('dp'), may hold values from -3 to 3
- cell_weight: bfloat16 [1280, 5120], P('dp'), may hold values from -0.15625 to 0.15625
- gene_weight: bfloat16 [1280, 5120], P('dp'), may hold values from -0.15625 to 0.15625
- decoder_bias: bfloat16 [5120], P('dp'), may hold values from -3 to 3
- readout: bfloat16 [5120], P('dp'), may hold values from -0.15625 to 0.15625
- gene_embed: bfloat16 [2, 32, 384, 1280], P(None, ('dp', 'query')), may hold values from -6 to 6
- query_cell: int32 [2, 32, 384], P(None, ('dp', 'query')), may hold values from 0 to 1
- query_label: int32 [2, 32, 384], P(None, ('dp', 'query')), may hold values 0 or 1
- query_live: int32 [16, 2, 2], P('dp', None, 'query'), may hold values from 1 to 384, 480 in all within a row
Outputs:
- block_out: bfloat16 [2, 32, 128, 1280], P(None, ('dp', 'query'))
- grad_tokens: float32 [2, 32, 128, 1280], P(None, ('dp', 'query'))
- grad_qkv: float32 [1280, 3840], P('dp')
- grad_out: float32 [1280, 1280], P('dp')
- grad_up: float32 [1280, 5120], P('dp')
- grad_down: float32 [5120, 1280], P('dp')
- grad_attn_gain: float32 [1280], P('dp')
- grad_ffn_gain: float32 [1280], P('dp')
- grad_up_bias: float32 [5120], P('dp')
- grad_cell: float32 [1280, 5120], P('dp')
- grad_gene: float32 [1280, 5120], P('dp')
- grad_decoder_bias: float32 [5120], P('dp')
- grad_readout: float32 [5120], P('dp')
Inputs may be any that keep to these rules, and one draw needn't show every extreme that they name: `query_live`: the 2 devices of one dp index together hold 480 live rows in each micro-batch; a device's live rows are its first slots. `query_cell`: index of a cell within the query group of the row's device.
All inputs are finite; a program needn't handle non-finite values. No bound on the sum of `query_label` on one device may be relied on, other than what follows from the above.
Results may differ from a plain program's by a relative error of at most 0.02.
Values may be sent and summed in bfloat16 or wider, within the bound.
No kernel may reach another device: no remote copies, remote signals or barrier semaphores. Data moves between devices by JAX's collectives and lax.ppermute only.
A program may use at most 320 MiB of HBM per device.

v0:
```python
import jax
import jax.numpy as jnp
from jax import lax
from jax.sharding import PartitionSpec as P

D = 1280
HEADS = 20
HEAD = 64
highest = lax.Precision.HIGHEST
epsilon = 1e-05


def row_product(left, right):
    return lax.dot_general(
        left, right, (((0,), (0,)), ((), ())), preferred_element_type=jnp.float32
    )


def times_transpose(left, right):
    return lax.dot_general(
        left, right, (((1,), (1,)), ((), ())), preferred_element_type=jnp.float32
    )


def layer_stats(values):
    average = jnp.mean(values, axis=-1, keepdims=True)
    centred = values - average
    variance = jnp.mean(centred * centred, axis=-1, keepdims=True)
    inverse = lax.rsqrt(variance + epsilon)
    return (centred * inverse, inverse)


def norm_back(grad_scaled, gain, normal, inverse):
    grad_normal = grad_scaled * gain
    along_normal = jnp.mean(grad_normal * normal, axis=-1, keepdims=True)
    average = jnp.mean(grad_normal, axis=-1, keepdims=True)
    grad_values = inverse * (grad_normal - average - normal * along_normal)
    return (grad_values, jnp.sum(grad_scaled * normal, axis=0))


def encode(inputs, weights):
    qkv_weight, out_weight, up_weight, down_weight, attn_gain, ffn_gain, up_bias = weights
    length = inputs.shape[0]
    tokens_wide = inputs.astype(jnp.float32)
    norm_one, scale_one = layer_stats(tokens_wide)
    normed = (norm_one * attn_gain.astype(jnp.float32)).astype(jnp.bfloat16)
    projected = jnp.dot(normed, qkv_weight, preferred_element_type=jnp.float32).astype(jnp.bfloat16)
    projected = projected.reshape(length, 3, HEADS, HEAD)
    queries = projected[:, 0]
    key_heads = projected[:, 1]
    value_heads = projected[:, 2]
    scores = (
        jnp.einsum("qhd,khd->hqk", queries, key_heads, preferred_element_type=jnp.float32) * 0.125
    )
    row_max = jnp.max(scores, axis=-1, keepdims=True)
    shifted = jnp.exp(scores - row_max)
    row_total = jnp.sum(shifted, axis=-1, keepdims=True)
    attn_probs = (shifted / row_total).astype(jnp.bfloat16)
    logsum = row_max + jnp.log(row_total)
    mixed_heads = jnp.einsum(
        "hqk,khd->qhd", attn_probs, value_heads, preferred_element_type=jnp.float32
    )
    mixed_heads = mixed_heads.astype(jnp.bfloat16).reshape(length, D)
    hidden = tokens_wide + jnp.dot(mixed_heads, out_weight, preferred_element_type=jnp.float32)
    norm_two, scale_two = layer_stats(hidden)
    second = (norm_two * ffn_gain.astype(jnp.float32)).astype(jnp.bfloat16)
    up_proj = jnp.dot(second, up_weight, preferred_element_type=jnp.float32) + up_bias.astype(
        jnp.float32
    )
    active = jax.nn.gelu(up_proj, approximate=True).astype(jnp.bfloat16)
    output = hidden + jnp.dot(active, down_weight, preferred_element_type=jnp.float32)
    saved_state = (
        norm_one,
        scale_one,
        normed,
        queries,
        key_heads,
        value_heads,
        logsum,
        mixed_heads,
        norm_two,
        scale_two,
        second,
        up_proj,
        active,
    )
    return (output, saved_state)


def encode_back(grad_output, saved_state, weights):
    qkv_weight, out_weight, up_weight, down_weight, attn_gain, ffn_gain = weights
    (
        norm_one,
        scale_one,
        normed,
        queries,
        key_heads,
        value_heads,
        logsum,
        mixed_heads,
        norm_two,
        scale_two,
        second,
        up_proj,
        active,
    ) = saved_state
    length = grad_output.shape[0]
    grad_branch = grad_output.astype(jnp.bfloat16)
    grad_down = row_product(active, grad_branch)
    grad_active = times_transpose(grad_branch, down_weight)
    gelu_back = jax.vjp(lambda inner_values: jax.nn.gelu(inner_values, approximate=True), up_proj)[
        1
    ]
    grad_up_proj = gelu_back(grad_active)[0].astype(jnp.bfloat16)
    grad_up = row_product(second, grad_up_proj)
    grad_up_bias = jnp.sum(grad_up_proj.astype(jnp.float32), axis=0)
    grad_second = times_transpose(grad_up_proj, up_weight)
    grad_hidden_norm, grad_ffn_gain = norm_back(
        grad_second, ffn_gain.astype(jnp.float32), norm_two, scale_two
    )
    grad_hidden = grad_output + grad_hidden_norm
    grad_attn = grad_hidden.astype(jnp.bfloat16)
    grad_out = row_product(mixed_heads, grad_attn)
    grad_mixed = (
        times_transpose(grad_attn, out_weight).astype(jnp.bfloat16).reshape(length, HEADS, HEAD)
    )
    scores = (
        jnp.einsum("qhd,khd->hqk", queries, key_heads, preferred_element_type=jnp.float32) * 0.125
    )
    attn_probs = jnp.exp(scores - logsum)
    probs_low = attn_probs.astype(jnp.bfloat16)
    grad_values = jnp.einsum(
        "hqk,qhd->khd", probs_low, grad_mixed, preferred_element_type=jnp.float32
    )
    grad_probs = jnp.einsum(
        "qhd,khd->hqk", grad_mixed, value_heads, preferred_element_type=jnp.float32
    )
    along_probs = jnp.sum(grad_probs * attn_probs, axis=-1, keepdims=True)
    grad_scores = (attn_probs * (grad_probs - along_probs) * 0.125).astype(jnp.bfloat16)
    grad_queries = jnp.einsum(
        "hqk,khd->qhd", grad_scores, key_heads, preferred_element_type=jnp.float32
    )
    grad_keys = jnp.einsum("hqk,qhd->khd", grad_scores, queries, preferred_element_type=jnp.float32)
    grad_projected = (
        jnp.stack([grad_queries, grad_keys, grad_values], axis=1)
        .astype(jnp.bfloat16)
        .reshape(length, 3 * D)
    )
    grad_qkv = row_product(normed, grad_projected)
    grad_normed = times_transpose(grad_projected, qkv_weight)
    grad_input_norm, grad_attn_gain = norm_back(
        grad_normed, attn_gain.astype(jnp.float32), norm_one, scale_one
    )
    grad_input = grad_hidden + grad_input_norm
    return (
        (grad_qkv, grad_out, grad_up, grad_down, grad_attn_gain, grad_ffn_gain, grad_up_bias),
        grad_input,
    )


def decode(summary_all, weights, gene_rows, cell_ids, labels, live_count):
    cell_weight, gene_weight, decoder_bias, readout = weights
    group_size = summary_all.shape[0]
    slot_count = gene_rows.shape[0]
    cell_part = jnp.dot(summary_all, cell_weight, preferred_element_type=jnp.float32)
    onehot = (cell_ids[:, None] == jnp.arange(group_size, dtype=jnp.int32)[None, :]).astype(
        jnp.float32
    )
    picked = jnp.dot(onehot, cell_part, precision=highest)
    pre_act = (
        picked
        + jnp.dot(gene_rows, gene_weight, preferred_element_type=jnp.float32)
        + decoder_bias.astype(jnp.float32)
    )
    activity, silu_back = jax.vjp(jax.nn.silu, pre_act)
    read_wide = readout.astype(jnp.float32)
    logits = jnp.sum(activity * read_wide[None, :], axis=-1)
    live_rows = (jnp.arange(slot_count, dtype=jnp.int32) < live_count).astype(jnp.float32)
    grad_logits = live_rows * (jax.nn.sigmoid(logits) - labels.astype(jnp.float32))
    grad_readout = jnp.sum(grad_logits[:, None] * activity, axis=0)
    grad_pre = silu_back(grad_logits[:, None] * read_wide[None, :])[0].astype(jnp.bfloat16)
    grad_pre_wide = grad_pre.astype(jnp.float32)
    grad_decoder_bias = jnp.sum(grad_pre_wide, axis=0)
    grad_gene = row_product(gene_rows, grad_pre)
    grad_cellproj = lax.dot_general(
        onehot, grad_pre_wide, (((0,), (0,)), ((), ())), precision=highest
    )
    grad_cell = lax.dot_general(
        summary_all.astype(jnp.float32), grad_cellproj, (((0,), (0,)), ((), ())), precision=highest
    )
    grad_summary = lax.dot_general(
        grad_cellproj, cell_weight.astype(jnp.float32), (((1,), (1,)), ((), ())), precision=highest
    )
    return ((grad_cell, grad_gene, grad_decoder_bias, grad_readout), grad_summary)


def shards(
    tokens,
    out_cotangent,
    qkv_weight,
    out_weight,
    up_weight,
    down_weight,
    attn_gain,
    ffn_gain,
    up_bias,
    cell_weight,
    gene_weight,
    decoder_bias,
    readout,
    gene_embed,
    query_cell,
    query_label,
    query_live,
):
    micro_count = tokens.shape[0]
    outputs = []
    input_grads = []
    totals = None
    for micro_index in range(micro_count):
        gathered = (
            lax.all_gather(qkv_weight, "dp", axis=0, tiled=True),
            lax.all_gather(out_weight, "dp", axis=0, tiled=True),
            lax.all_gather(up_weight, "dp", axis=0, tiled=True),
            lax.all_gather(down_weight, "dp", axis=0, tiled=True),
            lax.all_gather(attn_gain, "dp", axis=0, tiled=True),
            lax.all_gather(ffn_gain, "dp", axis=0, tiled=True),
            lax.all_gather(up_bias, "dp", axis=0, tiled=True),
            lax.all_gather(cell_weight, "dp", axis=0, tiled=True),
            lax.all_gather(gene_weight, "dp", axis=0, tiled=True),
            lax.all_gather(decoder_bias, "dp", axis=0, tiled=True),
            lax.all_gather(readout, "dp", axis=0, tiled=True),
        )
        output, saved_state = encode(tokens[micro_index, 0], gathered[:7])
        outputs.append(output.astype(jnp.bfloat16))
        summary_all = lax.all_gather(output[0:1].astype(jnp.bfloat16), "query", axis=0, tiled=True)
        decoder_grads, grad_summary = decode(
            summary_all,
            gathered[7:],
            gene_embed[micro_index, 0],
            query_cell[micro_index, 0],
            query_label[micro_index, 0],
            query_live[0, micro_index, 0],
        )
        grad_own = lax.psum_scatter(
            grad_summary.astype(jnp.bfloat16), "query", scatter_dimension=0, tiled=True
        ).astype(jnp.float32)
        grad_output = out_cotangent[micro_index, 0].astype(jnp.float32)
        grad_output = grad_output.at[0:1].add(grad_own)
        back_weights = (
            lax.all_gather(qkv_weight, "dp", axis=0, tiled=True),
            lax.all_gather(out_weight, "dp", axis=0, tiled=True),
            lax.all_gather(up_weight, "dp", axis=0, tiled=True),
            lax.all_gather(down_weight, "dp", axis=0, tiled=True),
            lax.all_gather(attn_gain, "dp", axis=0, tiled=True),
            lax.all_gather(ffn_gain, "dp", axis=0, tiled=True),
        )
        encoder_grads, grad_input = encode_back(grad_output, saved_state, back_weights)
        input_grads.append(grad_input)
        step_grads = encoder_grads + decoder_grads
        if micro_index == 0:
            totals = tuple(step_grads)
        else:
            totals = tuple((earlier + later for earlier, later in zip(totals, step_grads)))
    owned = (
        lax.psum_scatter(
            totals[0].astype(jnp.bfloat16), "dp", scatter_dimension=0, tiled=True
        ).astype(jnp.float32),
        lax.psum_scatter(
            totals[1].astype(jnp.bfloat16), "dp", scatter_dimension=0, tiled=True
        ).astype(jnp.float32),
        lax.psum_scatter(
            totals[2].astype(jnp.bfloat16), "dp", scatter_dimension=0, tiled=True
        ).astype(jnp.float32),
        lax.psum_scatter(
            totals[3].astype(jnp.bfloat16), "dp", scatter_dimension=0, tiled=True
        ).astype(jnp.float32),
        lax.psum_scatter(
            totals[4].astype(jnp.bfloat16), "dp", scatter_dimension=0, tiled=True
        ).astype(jnp.float32),
        lax.psum_scatter(
            totals[5].astype(jnp.bfloat16), "dp", scatter_dimension=0, tiled=True
        ).astype(jnp.float32),
        lax.psum_scatter(
            totals[6].astype(jnp.bfloat16), "dp", scatter_dimension=0, tiled=True
        ).astype(jnp.float32),
        lax.psum_scatter(
            totals[7].astype(jnp.bfloat16), "dp", scatter_dimension=0, tiled=True
        ).astype(jnp.float32),
        lax.psum_scatter(
            totals[8].astype(jnp.bfloat16), "dp", scatter_dimension=0, tiled=True
        ).astype(jnp.float32),
        lax.psum_scatter(
            totals[9].astype(jnp.bfloat16), "dp", scatter_dimension=0, tiled=True
        ).astype(jnp.float32),
        lax.psum_scatter(
            totals[10].astype(jnp.bfloat16), "dp", scatter_dimension=0, tiled=True
        ).astype(jnp.float32),
    )
    totals = (
        lax.psum(owned[0].astype(jnp.bfloat16), "query").astype(jnp.float32),
        lax.psum(owned[1].astype(jnp.bfloat16), "query").astype(jnp.float32),
        lax.psum(owned[2].astype(jnp.bfloat16), "query").astype(jnp.float32),
        lax.psum(owned[3].astype(jnp.bfloat16), "query").astype(jnp.float32),
        lax.psum(owned[4].astype(jnp.bfloat16), "query").astype(jnp.float32),
        lax.psum(owned[5].astype(jnp.bfloat16), "query").astype(jnp.float32),
        lax.psum(owned[6].astype(jnp.bfloat16), "query").astype(jnp.float32),
        lax.psum(owned[7].astype(jnp.bfloat16), "query").astype(jnp.float32),
        lax.psum(owned[8].astype(jnp.bfloat16), "query").astype(jnp.float32),
        lax.psum(owned[9].astype(jnp.bfloat16), "query").astype(jnp.float32),
        lax.psum(owned[10].astype(jnp.bfloat16), "query").astype(jnp.float32),
    )
    block_out = jnp.stack(outputs, axis=0)[:, None]
    grad_tokens = jnp.stack(input_grads, axis=0)[:, None]
    return (
        block_out,
        grad_tokens,
        totals[0],
        totals[1],
        totals[2],
        totals[3],
        totals[4],
        totals[5],
        totals[6],
        totals[7],
        totals[8],
        totals[9],
        totals[10],
    )


def solution(mesh):
    placed = (
        P(None, ("dp", "query"), None, None),
        P(None, ("dp", "query"), None, None),
        P("dp", None),
        P("dp", None),
        P("dp", None),
        P("dp", None),
        P("dp"),
        P("dp"),
        P("dp"),
        P("dp", None),
        P("dp", None),
        P("dp"),
        P("dp"),
        P(None, ("dp", "query"), None, None),
        P(None, ("dp", "query"), None),
        P(None, ("dp", "query"), None),
        P("dp", None, "query"),
    )
    return jax.shard_map(
        shards,
        mesh=mesh,
        in_specs=placed,
        out_specs=(
            P(None, ("dp", "query"), None, None),
            P(None, ("dp", "query"), None, None),
            P("dp", None),
            P("dp", None),
            P("dp", None),
            P("dp", None),
            P("dp"),
            P("dp"),
            P("dp"),
            P("dp", None),
            P("dp", None),
            P("dp"),
            P("dp"),
        ),
        check_vma=False,
    )
```

profile of v0, /device:TPU:0, one launch (start us, length us, event | category | flops | bytes accessed | tf_op | source)
XLA Modules:
  0.0 1549.0 jit_solution(1948422574728645002)
XLA Ops:
  14.5 65.3 %all-reduce.13 = (bf16[1280]{0:T(1024)(128)(2,1)S(1)}, bf16[5120]{0:T(1024)(128)(2,1)S(1)}, bf16[1280]{0:T(1024)(128)(2,1)S(1)}, bf16[5120]{0:T(1024)(128)(2,1)S(1)}, bf16[5120]{0:T(1024)(128)(2,1)S(1)}) all-reduce(bf16[1280]{0:T(1024)(128)(2,1)S(1)} %dynamic-update-slice.6, ...), channel_id=1, replica_groups=mesh['dp'=16,'query'=2] {'dp'}, use_global_device_ids=true, to_apply=%add | all-reduce | flops 17920 | bytes 71680
  81.0 16.6 %all-gather.9.cloned.1.call-done = bf16[1280,3840]{1,0:T(8,128)(2,1)} async-done(((bf16[80,3840]{1,0:T(8,128)(2,1)}), bf16[1280,3840]{1,0:T(8,128)(2,1)}) %all-gather.9.cloned.1.call-update) | async-done | bytes 9830416 | tf_op jit(solution)/shard_map/all_gather | solution.py:222
  97.6 5.3 convolution_convert_fusion
  103.7 5.9 convolution_convert_fusion.1
  112.9 31.2 %all-gather.11.cloned.1.call-done = bf16[1280,1280]{1,0:T(8,128)(2,1)} async-done(((bf16[80,1280]{1,0:T(8,128)(2,1)}), bf16[1280,1280]{1,0:T(8,128)(2,1)}) %all-gather.11.cloned.1.call-update) | async-done | bytes 3276816 | tf_op jit(solution)/shard_map/all_gather | solution.py:223
  144.1 2.7 fusion.191
  151.0 98.3 %all-gather.13.cloned.1.call-done = bf16[1280,5120]{1,0:T(8,128)(2,1)} async-done(((bf16[80,5120]{1,0:T(8,128)(2,1)}), bf16[1280,5120]{1,0:T(8,128)(2,1)}) %all-gather.13.cloned.1.call-update) | async-done | bytes 13107216 | tf_op jit(solution)/shard_map/all_gather | solution.py:224
  249.3 8.2 convolution_add_fusion.1
  257.5 96.1 %all-gather.15.cloned.1.call-done = bf16[5120,1280]{1,0:T(8,128)(2,1)} async-done(((bf16[320,1280]{1,0:T(8,128)(2,1)}), bf16[5120,1280]{1,0:T(8,128)(2,1)}) %all-gather.15.cloned.1.call-update) | async-done | bytes 13107216 | tf_op jit(solution)/shard_map/all_gather | solution.py:225
  353.6 8.0 fusion.27
  361.6 4.7 all-gather.1
  366.3 2.0 convolution_add_fusion.2
  368.4 2.4 fusion.26
  370.8 4.4 all-gather
  375.1 82.8 %all-gather.17.cloned.1.call-done = bf16[1280,5120]{1,0:T(8,128)(2,1)} async-done(((bf16[80,5120]{1,0:T(8,128)(2,1)}), bf16[1280,5120]{1,0:T(8,128)(2,1)}) %all-gather.17.cloned.1.call-update) | async-done | bytes 13107216 | tf_op jit(solution)/shard_map/all_gather | solution.py:229
  457.9 6.5 fusion.165
  464.5 97.8 %all-gather.19.cloned.1.call-done = bf16[1280,5120]{1,0:T(8,128)(2,1)} async-done(((bf16[80,5120]{1,0:T(8,128)(2,1)}), bf16[1280,5120]{1,0:T(8,128)(2,1)}) %all-gather.19.cloned.1.call-update) | async-done | bytes 13107216 | tf_op jit(solution)/shard_map/all_gather | solution.py:230
  562.3 10.5 fusion.49
  572.8 6.2 add_add_fusion
  579.1 12.6 fusion.53
  591.8 1.8 fusion.169
  593.6 9.9 multiply_reduce_fusion.3
  604.8 11.1 convert_reduce_fusion.1
  615.9 12.7 fusion.51
  628.6 16.2 %fusion.2 = bf16[1280,5120]{0,1:T(8,128)(2,1)} fusion(f32[5120,1280]{1,0:T(8,128)} %fusion.51, bf16[384,5120]{1,0:T(8,128)(2,1)} %get-tuple-element.137, bf16[2,1,384,1280]{3,2,1,0:T(8,128)(2,1)} %param.34), kind=kOutput, calls=%fused_computation.7 | convolution fusion | flops 5046272000 | bytes 44236800 | tf_op jit(solution)/shard_map/dot_general | solution.py:14
  644.8 17.6 %copy.89 = bf16[1280,5120]{1,0:T(8,128)(2,1)} copy(bf16[1280,5120]{0,1:T(8,128)(2,1)} %fusion.2) | data formatting | bytes 26214400
  663.7 2.1 slice_convert_fusion.1
  665.8 3.1 fusion.135
  670.4 14.2 convolution_convert_fusion.5
  684.5 13.5 convolution_convert_fusion.4
  698.0 8.3 all-reduce.15
  708.9 11.2 convert_reduce_fusion.3
  720.1 10.6 multiply_reduce_fusion.7
  730.7 9.7 convert_reduce_fusion.2
  740.5 10.3 multiply_reduce_fusion.6
  753.1 2.7 fusion.11
  757.7 3.0 convolution_convert_fusion.3
  760.8 1.9 copy.70
  762.6 3.0 convolution_convert_fusion.2
  769.5 2.2 convolution_bitcast_fusion.5
  771.7 3.2 convolution_bitcast_fusion.4
  774.9 2.4 fusion.133
  777.3 3.1 convolution_bitcast_fusion.2
  780.4 3.1 convolution_bitcast_fusion.1
  786.1 8.3 fusion.116
  794.5 11.1 add_convert_fusion.4
  806.7 12.7 fusion.185
  819.5 15.7 %add_convert_fusion.3 = bf16[1280,5120]{1,0:T(8,128)(2,1)} fusion(f32[1280,5120]{1,0:T(8,128)} %fusion.185, bf16[128,5120]{1,0:T(8,128)(2,1)} %copy-done.26, f32[128,1280]{1,0:T(8,128)S(1)} %copy-done.6, f32[128]{0:T(128)S(1)} %copy-done.75, f32[128]{0:T(128)S(1)} %copy-done.70, f32[1280]{0:T(1024)S(1)} %convert_element_type.331), kind=kOutput, calls=%fused_computation.5 | convolution fusion | flops 1691484160 | bytes 41293824 | tf_op jit(solution)/shard_map/dot_general | solution.py:14
  836.3 12.8 fusion.146
  849.1 16.3 %add_convert_fusion.2 = bf16[5120,1280]{1,0:T(8,128)(2,1)} fusion(f32[5120,1280]{1,0:T(8,128)} %fusion.146, f32[128,1280]{1,0:T(8,128)S(1)} %copy-done.22, f32[128,5120]{1,0:T(8,128)} %convolution_add_fusion.1), kind=kOutput, calls=%fused_computation.4 | convolution fusion | flops 1696890880 | bytes 42598400 | tf_op jit(solution)/shard_map/dot_general | solution.py:14
  866.1 13.9 fusion.167
  880.0 19.8 %add_convert_fusion.1 = bf16[1280,5120]{1,0:T(8,128)(2,1)} fusion(f32[1280,5120]{1,0:T(8,128)} %fusion.167, f32[2,5120]{1,0:T(2,128)S(1)} %fusion.134, bf16[2,1,1280]{2,1,0:T(2,128)(2,1)S(1)} %copy-done.61), kind=kOutput, calls=%fused_computation.3 | convolution fusion | flops 170393600 | bytes 39367680 | tf_op jit(solution)/shard_map/dot_general | solution.py:188
  901.2 2.3 copy.90
  903.5 83.3 %reduce-scatter.9.cloned.1.call-done = bf16[80,3840]{1,0:T(8,128)(2,1)} async-done(((bf16[1280,3840]{1,0:T(8,128)(2,1)}), bf16[80,3840]{1,0:T(8,128)(2,1)}) %reduce-scatter.9.cloned.1.call-update) | async-done | bytes 614416 | tf_op jit(solution)/shard_map/reduce_scatter | solution.py:266
  986.8 142.1 %reduce-scatter.13.cloned.1.call-done = bf16[80,5120]{1,0:T(8,128)(2,1)} async-done(((bf16[1280,5120]{1,0:T(8,128)(2,1)}), bf16[80,5120]{1,0:T(8,128)(2,1)}) %reduce-scatter.13.cloned.1.call-update) | async-done | bytes 819216 | tf_op jit(solution)/shard_map/reduce_scatter | solution.py:272
  1128.9 142.2 %reduce-scatter.15.cloned.1.call-done = bf16[320,1280]{1,0:T(8,128)(2,1)} async-done(((bf16[5120,1280]{1,0:T(8,128)(2,1)}), bf16[320,1280]{1,0:T(8,128)(2,1)}) %reduce-scatter.15.cloned.1.call-update) | async-done | bytes 819216 | tf_op jit(solution)/shard_map/reduce_scatter | solution.py:275
  1271.1 141.5 %reduce-scatter.17.cloned.1.call-done = bf16[80,5120]{1,0:T(8,128)(2,1)} async-done(((bf16[1280,5120]{1,0:T(8,128)(2,1)}), bf16[80,5120]{1,0:T(8,128)(2,1)}) %reduce-scatter.17.cloned.1.call-update) | async-done | bytes 819216 | tf_op jit(solution)/shard_map/reduce_scatter | solution.py:287
  1412.6 7.2 fusion.194
  1419.9 8.4 fusion.81
  1428.5 59.6 %all-reduce.12 = (bf16[1280]{0:T(1024)(128)(2,1)S(1)}, bf16[1280]{0:T(1024)(128)(2,1)S(1)}, bf16[5120]{0:T(1024)(128)(2,1)S(1)}, bf16[5120]{0:T(1024)(128)(2,1)S(1)}, bf16[5120]{0:T(1024)(128)(2,1)S(1)}) all-reduce(bf16[1280]{0:T(1024)(128)(2,1)S(1)} %add_convert_fusion.9, ...), channel_id=8, replica_groups=mesh['dp'=16,'query'=2] {'dp'}, use_global_device_ids=true, to_apply=%region_36.37.clone | all-reduce | flops 17920 | bytes 71680
  1488.5 5.0 all-reduce.14
  1497.2 1.6 fusion.80
  1499.9 33.9 %all-reduce.19.cloned.1.call-done = (bf16[80,5120]{0,1:T(8,128)(2,1)}, bf16[80,3840]{1,0:T(8,128)(2,1)}, bf16[80,1280]{1,0:T(8,128)(2,1)}, bf16[80,5120]{1,0:T(8...) async-done(((bf16[80,5120]{0,1:T(8,128)(2,1)}, bf16[80,3840]{1,0:T(8,128)(2,1)}, bf16[80,1280]{1,0:T(8,128)(2,1)}, bf16[80,5120]{1,0:T(8,128)(2,1)}, ...) | async-done | bytes 4096016 | tf_op jit(solution)/shard_map/psum | solution.py:309
  1533.8 2.6 convert_element_type.387
  (319 shorter events, 46.4 us)
Async XLA Ops:
  7.2 72.5 %copy-start.85 = (s32[1,2,1]{1,2,0:T(1,128)S(1)}, s32[1,2,1]{1,2,0:T(1,128)}, u32[]{:S(2)}) copy-start(s32[1,2,1]{1,2,0:T(1,128)} %param.37) | copy-start | bytes 28
  7.3 73.1 %copy-start.82 = (s32[2,1,384]{2,1,0:T(1,128)S(1)}, s32[2,1,384]{2,1,0:T(1,128)}, u32[]{:S(2)}) copy-start(s32[2,1,384]{2,1,0:T(1,128)} %param.35) | copy-start | bytes 9220
  7.3 73.1 %copy-start.83 = (s32[2,1,384]{2,1,0:T(1,128)S(1)}, s32[2,1,384]{2,1,0:T(1,128)}, u32[]{:S(2)}) copy-start(s32[2,1,384]{2,1,0:T(1,128)} %param.36) | copy-start | bytes 9220
  7.3 73.2 %copy-start.7 = (bf16[2,1,128,1280]{3,2,1,0:T(8,128)(2,1)S(1)}, bf16[2,1,128,1280]{3,2,1,0:T(8,128)(2,1)}, u32[]{:S(2)}) copy-start(bf16[2,1,128,1280]{3,2,1,0:T(8,128)(2,1)} %param.21) | copy-start | bytes 1966084
  7.3 90.3 %all-gather.9.cloned.1.call-start = ((), (), s32[]{:S(2)}) async-start(), calls=%async_computation.6 | async-start | bytes 10444800 | tf_op jit(solution)/shard_map/all_gather | solution.py:222
  8.0 136.1 %all-gather.11.cloned.1.call-start = ((), (), s32[]{:S(2)}) async-start(), calls=%async_computation.7 | async-start | bytes 3481600 | tf_op jit(solution)/shard_map/all_gather | solution.py:223
  8.8 240.5 %all-gather.13.cloned.1.call-start = ((), (), s32[]{:S(2)}) async-start(), calls=%async_computation.8 | async-start | bytes 13926400 | tf_op jit(solution)/shard_map/all_gather | solution.py:224
  9.5 344.1 %all-gather.15.cloned.1.call-start = ((), (), s32[]{:S(2)}) async-start(), calls=%async_computation.9 | async-start | bytes 13926400 | tf_op jit(solution)/shard_map/all_gather | solution.py:225
  10.1 447.9 %all-gather.17.cloned.1.call-start = ((), (), s32[]{:S(2)}) async-start(), calls=%async_computation.10 | async-start | bytes 13926400 | tf_op jit(solution)/shard_map/all_gather | solution.py:229
  10.7 551.6 %all-gather.19.cloned.1.call-start = ((), (), s32[]{:S(2)}) async-start(), calls=%async_computation.11 | async-start | bytes 13926400 | tf_op jit(solution)/shard_map/all_gather | solution.py:230
  11.2 889.9 %reduce-scatter.19.cloned.1.call-start = ((), (), s32[]{:S(2)}) async-start(), calls=%async_computation.17 | async-start | bytes 13926400
  79.8 23.9 %copy-start.43 = (f32[1280]{0:T(1024)}, f32[1280]{0:T(1024)S(1)}, u32[]{:S(2)}) copy-start(f32[1280]{0:T(1024)S(1)} %convert_element_type.325) | copy-start | bytes 15364
  80.6 22.3 %copy-start.76 = (f32[128]{0:T(128)}, f32[128]{0:T(128)S(1)}, u32[]{:S(2)}) copy-start(f32[128]{0:T(128)S(1)} %get-tuple-element.159) | copy-start | bytes 1540
  80.6 23.0 %copy-start.71 = (f32[128]{0:T(128)}, f32[128]{0:T(128)S(1)}, u32[]{:S(2)}) copy-start(f32[128]{0:T(128)S(1)} %get-tuple-element.160) | copy-start | bytes 1540
  81.0 22.0 %copy-start.80 = (f32[128]{0:T(128)}, f32[128]{0:T(128)S(1)}, u32[]{:S(2)}) copy-start(f32[128]{0:T(128)S(1)} %add_rsqrt_fusion.1) | copy-start | bytes 1540
  81.0 22.6 %copy-start.78 = (f32[128]{0:T(128)}, f32[128]{0:T(128)S(1)}, u32[]{:S(2)}) copy-start(f32[128]{0:T(128)S(1)} %add_rsqrt_fusion.3) | copy-start | bytes 1540
  112.9 34.1 %copy-start.38 = (bf16[20,64,128]{2,1,0:T(8,128)(2,1)}, bf16[20,64,128]{2,1,0:T(8,128)(2,1)S(1)}, u32[]{:S(2)}) copy-start(bf16[20,64,128]{2,1,0:T(8,128)(2,1)S(1)} %convolution_convert_fusion.6) | copy-start | bytes 983044
  146.8 605.1 %copy-start.5 = (f32[128,1280]{1,0:T(8,128)}, f32[128,1280]{1,0:T(8,128)S(1)}, u32[]{:S(2)}) copy-start(f32[128,1280]{1,0:T(8,128)S(1)} %get-tuple-element.146) | copy-start | bytes 1966084
  146.8 102.5 %copy-start.69 = (f32[128]{0:T(128)}, f32[128]{0:T(128)S(1)}, u32[]{:S(2)}) copy-start(f32[128]{0:T(128)S(1)} %broadcast_multiply_fusion.8) | copy-start | bytes 1540
  150.7 589.7 %copy-start.9 = (f32[128,1280]{1,0:T(8,128)}, f32[128,1280]{1,0:T(8,128)S(1)}, u32[]{:S(2)}) copy-start(f32[128,1280]{1,0:T(8,128)S(1)} %get-tuple-element.150) | copy-start | bytes 1966084
  151.0 106.5 %copy-start.74 = (f32[128]{0:T(128)}, f32[128]{0:T(128)S(1)}, u32[]{:S(2)}) copy-start(f32[128]{0:T(128)S(1)} %add_rsqrt_fusion) | copy-start | bytes 1540
  353.6 12.7 copy-start
  353.6 14.7 slice-start.4
  353.6 14.7 slice-start.5
  353.6 14.7 slice-start.6
  366.3 91.6 %copy-start.60 = (bf16[2,1,1280]{2,1,0:T(2,128)(2,1)}, bf16[2,1,1280]{2,1,0:T(2,128)(2,1)S(1)}, u32[]{:S(2)}) copy-start(bf16[2,1,1280]{2,1,0:T(2,128)(2,1)S(1)} %all-gather.1) | copy-start | bytes 15364
  370.8 93.7 %copy-start.47 = (bf16[128,1280]{1,0:T(8,128)(2,1)}, bf16[128,1280]{1,0:T(8,128)(2,1)S(1)}, u32[]{:S(2)}) copy-start(bf16[128,1280]{1,0:T(8,128)(2,1)S(1)} %fusion.26) | copy-start | bytes 983044
  375.1 216.6 %copy-start.62 = (bf16[2,1,1280]{2,1,0:T(2,128)(2,1)}, bf16[2,1,1280]{2,1,0:T(2,128)(2,1)S(1)}, u32[]{:S(2)}) copy-start(bf16[2,1,1280]{2,1,0:T(2,128)(2,1)S(1)} %all-gather) | copy-start | bytes 15364
  572.8 18.9 %slice-start = ((s8[13107200]{0:T(1024)(128)(4,1)}), s8[4194304]{0:T(1024)(128)(4,1)S(1)}, s32[]{:S(2)}) async-start(s8[13107200]{0:T(1024)(128)(4,1)} %bitcast.251), calls=%async_computation.19 | async-start | bytes 8388608
  572.8 18.9 %slice-start.1 = ((s8[13107200]{0:T(1024)(128)(4,1)}), s8[4194304]{0:T(1024)(128)(4,1)S(1)}, s32[]{:S(2)}) async-start(s8[13107200]{0:T(1024)(128)(4,1)} %bitcast.251), calls=%async_computation.20 | async-start | bytes 8388608
  579.1 12.7 slice-start.2
  579.1 12.7 slice-start.3
  615.9 12.7 copy-start.4
  662.5 241.1 %reduce-scatter.11.cloned.1.call-start = ((), (), s32[]{:S(2)}) async-start(), calls=%async_computation.13 | async-start | bytes 3481600 | tf_op jit(solution)/shard_map/reduce_scatter | solution.py:269
  707.9 44.0 %copy-start.21 = (f32[128,1280]{1,0:T(8,128)}, f32[128,1280]{1,0:T(8,128)S(1)}, u32[]{:S(2)}) copy-start(f32[128,1280]{1,0:T(8,128)S(1)} %scatter-add.9) | copy-start | bytes 1966084
  708.9 31.6 %copy-start.23 = (f32[128,1280]{1,0:T(8,128)}, f32[128,1280]{1,0:T(8,128)S(1)}, u32[]{:S(2)}) copy-start(f32[128,1280]{1,0:T(8,128)S(1)} %scatter-add.6) | copy-start | bytes 1966084
  720.1 10.6 copy-start.25
  720.1 10.6 copy-start.11
  730.7 9.8 copy-start.70
  730.7 9.8 copy-start.75
  740.5 10.4 copy-start.26
  740.5 10.4 copy-start.34
  755.8 231.0 %reduce-scatter.9.cloned.1.call-start = ((), (), s32[]{:S(2)}) async-start(), calls=%async_computation.12 | async-start | bytes 10444800 | tf_op jit(solution)/shard_map/reduce_scatter | solution.py:266
  785.4 9.1 copy-start.27
  786.1 8.4 copy-start.77
  786.1 8.4 copy-start.81
  805.6 13.8 copy-start.6
  805.7 323.3 %reduce-scatter.13.cloned.1.call-start = ((), (), s32[]{:S(2)}) async-start(), calls=%async_computation.14 | async-start | bytes 13926400 | tf_op jit(solution)/shard_map/reduce_scatter | solution.py:272
  835.2 13.9 copy-start.22
  835.2 435.9 %reduce-scatter.15.cloned.1.call-start = ((), (), s32[]{:S(2)}) async-start(), calls=%async_computation.15 | async-start | bytes 13926400 | tf_op jit(solution)/shard_map/reduce_scatter | solution.py:275
  865.4 14.6 copy-start.61
  865.4 547.1 %reduce-scatter.17.cloned.1.call-start = ((), (), s32[]{:S(2)}) async-start(), calls=%async_computation.16 | async-start | bytes 13926400 | tf_op jit(solution)/shard_map/reduce_scatter | solution.py:287
  899.8 633.9 %all-reduce.19.cloned.1.call-start = ((), (), s32[]{:S(2)}) async-start(), calls=%async_computation.18 | async-start | bytes 9175040 | tf_op jit(solution)/shard_map/psum | solution.py:309
  1419.8 8.5 copy-start.32
  1419.8 8.5 copy-start.68
  1419.8 8.5 copy-start.73
  1419.8 8.6 copy-start.58
  1419.8 8.6 copy-start.59
  1419.9 8.6 copy-start.56
  1419.9 8.6 copy-start.57
  1419.9 76.4 %copy-start.46 = (bf16[128,1280]{1,0:T(8,128)(2,1)S(1)}, bf16[128,1280]{1,0:T(8,128)(2,1)}, u32[]{:S(2)}) copy-start(bf16[128,1280]{1,0:T(8,128)(2,1)} %copy-done.45) | copy-start | bytes 983044
  1419.9 76.4 %copy-start.48 = (bf16[128,1280]{1,0:T(8,128)(2,1)S(1)}, bf16[128,1280]{1,0:T(8,128)(2,1)}, u32[]{:S(2)}) copy-start(bf16[128,1280]{1,0:T(8,128)(2,1)} %copy-done.47) | copy-start | bytes 983044
  1419.9 77.3 %copy-start.18 = (f32[128,1280]{1,0:T(8,128)S(1)}, f32[128,1280]{1,0:T(8,128)}, u32[]{:S(2)}) copy-start(f32[128,1280]{1,0:T(8,128)} %copy-done.17) | copy-start | bytes 1966084
  1419.9 77.2 %copy-start.20 = (f32[128,1280]{1,0:T(8,128)S(1)}, f32[128,1280]{1,0:T(8,128)}, u32[]{:S(2)}) copy-start(f32[128,1280]{1,0:T(8,128)} %copy-done.19) | copy-start | bytes 1966084
  (49 other events, 146.2 us)
Sparse Core Ops, SparseCore 0:
  10.4 87.1 all-gather.8
  99.9 44.1 all-gather.10
  146.4 102.8 all-gather.12
  251.4 102.1 all-gather.14
  355.7 102.1 all-gather.16
  460.1 102.1 all-gather.18
  662.6 136.5 reduce-scatter.18
  803.4 65.9 reduce-scatter.10
  873.6 113.2 reduce-scatter.8
  990.8 138.1 reduce-scatter.12
  1133.6 137.4 reduce-scatter.14
  1275.1 137.4 reduce-scatter.16
  1416.4 117.3 all-reduce.18
where the time goes:
time: 1560 us; the launch traced here: 1550 us
  waiting for transfers between devices  969 us (62%)
  matrix products  339 us (22%)
  blocking collectives  147 us (9%)
  local copies, waits for them, and re-layouts  41 us (3%)
  other arithmetic  33.2 us (2%)
  between operations  18 us (1%)
    reduce_scatter x1, waiting for transfers between devices, shards(): lax.psum_scatter(totals[3].astype(jnp.bfloat16), 'dp', scatter_dimension=...  142 us
    reduce_scatter x1, waiting for transfers between devices, shards(): lax.psum_scatter(totals[2].astype(jnp.bfloat16), 'dp', scatter_dimension=...  142 us
    reduce_scatter x1, waiting for transfers between devices, shards(): lax.psum_scatter(totals[7].astype(jnp.bfloat16), 'dp', scatter_dimension=...  141 us
    unnamed x3, blocking collectives  133 us
    dot_general x10, matrix products, row_product(): lax.dot_general(left, right, (((0,), (0,)), ((), ())), preferred_element_...  110 us
    all_gather x1, waiting for transfers between devices, shards(): lax.all_gather(up_weight, 'dp', axis=0, tiled=True)  98.3 us
    all_gather x1, waiting for transfers between devices, shards(): lax.all_gather(gene_weight, 'dp', axis=0, tiled=True)  97.8 us
    all_gather x1, waiting for transfers between devices, shards(): lax.all_gather(down_weight, 'dp', axis=0, tiled=True)  96.1 us
  transfers between devices with their start and end apart: 13, of which 11 were waited for; matrix products, arithmetic and copies ran while one was open for 19% of the time, Pallas kernels for 0%

commit v1 on v0

--- a/solution.py
+++ b/solution.py
@@ -1,3 +1,4 @@
+import functools
 import jax
 import jax.numpy as jnp
 from jax import lax
@@ -8,6 +9,26 @@
 HEAD = 64
 highest = lax.Precision.HIGHEST
 epsilon = 1e-05
+
+
+def place_teams(a0, across):
+    all_rows = lax.axis_size(across)
+    then = lax.axis_index(across)
+    arr_next, w1 = (all_rows, then)
+    res, y_new = (a0, 1)
+    while y_new < arr_next:
+        current_block = range(arr_next)
+        piece_now = map(lambda h: (h, h ^ y_new), current_block)
+        val2 = list(piece_now)
+        before = lax.ppermute(res, across, val2)
+        r_now = jnp.concatenate([res, before], axis=0)
+        val = jnp.concatenate([before, res], axis=0)
+        res = jnp.where(w1 & y_new == 0, r_now, val)
+        y_new = 2 * y_new
+    return res
+
+
+_apply_rounds = functools.partial(place_teams, across="dp")
 
 
 def row_product(left, right):
@@ -227,7 +248,7 @@
             lax.all_gather(ffn_gain, "dp", axis=0, tiled=True),
             lax.all_gather(up_bias, "dp", axis=0, tiled=True),
             lax.all_gather(cell_weight, "dp", axis=0, tiled=True),
-            lax.all_gather(gene_weight, "dp", axis=0, tiled=True),
+            _apply_rounds(gene_weight),
             lax.all_gather(decoder_bias, "dp", axis=0, tiled=True),
             lax.all_gather(readout, "dp", axis=0, tiled=True),
         )

time: 1560 us -> 1730 us (1.11)
  blocking collectives: 147 us -> 246 us
  waiting for transfers between devices: 969 us -> 1020 us
    unnamed x3, blocking collectives: 133 us -> 232 us
    all_gather x1 -> x0, waiting for transfers between devices: 97.8 us -> none  [shards(): lax.all_gather(gene_weight, 'dp', axis=0, tiled=True)]
    all_gather x1, waiting for transfers between devices: 98.3 us -> 173 us  [shards(): lax.all_gather(up_weight, 'dp', axis=0, tiled=True)]
    ppermute x0 -> x4, waiting for transfers between devices: none -> 51.6 us  [place_teams(): before = lax.ppermute(res, across, val2)]
    all_gather x1, waiting for transfers between devices: 96.1 us -> 135 us  [shards(): lax.all_gather(down_weight, 'dp', axis=0, tiled=True)]
    all_gather x1, waiting for transfers between devices: 82.8 us -> 116 us  [shards(): lax.all_gather(cell_weight, 'dp', axis=0, tiled=True)]
    all_gather x1, waiting for transfers between devices: 31.2 us -> 0.01 us  [shards(): lax.all_gather(out_weight, 'dp', axis=0, tiled=True)]
    unnamed x222 -> x246, local copies, waits for them, and re-layouts: 34.9 us -> 34.7 us
  transfers between devices with their start and end apart: 13 -> 16, of which waited for: 11 -> 10; matrix products, arithmetic and copies ran while one was open for 19% -> 19% of each run, Pallas kernels for 0% -> 0%
where the time goes in v1:
time: 1730 us
  waiting for transfers between devices  1020 us (59%)
  matrix products  343 us (20%)
  blocking collectives  246 us (14%)
  other arithmetic  48.1 us (3%)
  local copies, waits for them, and re-layouts  42.5 us (2%)
  between operations  18.7 us (1%)
    unnamed x3, blocking collectives  232 us
    all_gather x1, waiting for transfers between devices, shards(): lax.all_gather(up_weight, 'dp', axis=0, tiled=True)  173 us
    reduce_scatter x1, waiting for transfers between devices, shards(): lax.psum_scatter(totals[2].astype(jnp.bfloat16), 'dp', scatter_dimension=...  142 us
    reduce_scatter x1, waiting for transfers between devices, shards(): lax.psum_scatter(totals[3].astype(jnp.bfloat16), 'dp', scatter_dimension=...  142 us
    reduce_scatter x1, waiting for transfers between devices, shards(): lax.psum_scatter(totals[7].astype(jnp.bfloat16), 'dp', scatter_dimension=...  142 us
    all_gather x1, waiting for transfers between devices, shards(): lax.all_gather(down_weight, 'dp', axis=0, tiled=True)  135 us
    all_gather x1, waiting for transfers between devices, shards(): lax.all_gather(cell_weight, 'dp', axis=0, tiled=True)  116 us
    dot_general x10, matrix products, row_product(): lax.dot_general(left, right, (((0,), (0,)), ((), ())), preferred_element_...  110 us
  transfers between devices with their start and end apart: 16, of which 10 were waited for; matrix products, arithmetic and copies ran while one was open for 19% of the time, Pallas kernels for 0%

profile of v1, /device:TPU:0, one launch (start us, length us, event | category | flops | bytes accessed | tf_op | source)
XLA Modules:
  0.0 1725.6 jit_solution(849760421617607336)
XLA Ops:
  11.1 2.1 collective-permute-done
  15.0 3.0 collective-permute-start.1
  18.0 49.5 %collective-permute-done.1 = bf16[160,5120]{1,0:T(8,128)(2,1)} collective-permute-done((bf16[160,5120]{1,0:T(8,128)(2,1)S(1)}, bf16[160,5120]{1,0:T(8,128)(2,1)}, u32[]{:S(2)}, u32[]{:S(2)}) %collective-permute-start.1) | collective-permute-done | bytes 1638432 | tf_op jit(solution)/shard_map/ppermute | solution.py:23
  67.5 3.7 maximum_select_fusion.2
  75.9 163.8 %all-reduce.13 = (bf16[1280]{0:T(1024)(128)(2,1)S(1)}, bf16[5120]{0:T(1024)(128)(2,1)S(1)}, bf16[1280]{0:T(1024)(128)(2,1)S(1)}, bf16[5120]{0:T(1024)(128)(2,1)S(1)}, bf16[5120]{0:T(1024)(128)(2,1)S(1)}) all-reduce(bf16[1280]{0:T(1024)(128)(2,1)S(1)} %dynamic-update-slice.6, ...), channel_id=1, replica_groups=mesh['dp'=16,'query'=2] {'dp'}, use_global_device_ids=true, to_apply=%add | all-reduce | flops 17920 | bytes 71680
  241.0 8.2 maximum_select_fusion.1
  249.2 5.3 convolution_convert_fusion
  255.2 5.8 convolution_convert_fusion.1
  264.6 2.8 fusion.195
  271.7 172.6 %all-gather.12.cloned.1.call-done = bf16[1280,5120]{1,0:T(8,128)(2,1)} async-done(((bf16[80,5120]{1,0:T(8,128)(2,1)}), bf16[1280,5120]{1,0:T(8,128)(2,1)}) %all-gather.12.cloned.1.call-update) | async-done | bytes 13107216 | tf_op jit(solution)/shard_map/all_gather | solution.py:245
  444.3 8.2 convolution_add_fusion.1
  452.5 135.4 %all-gather.14.cloned.1.call-done = bf16[5120,1280]{1,0:T(8,128)(2,1)} async-done(((bf16[320,1280]{1,0:T(8,128)(2,1)}), bf16[5120,1280]{1,0:T(8,128)(2,1)}) %all-gather.14.cloned.1.call-update) | async-done | bytes 13107216 | tf_op jit(solution)/shard_map/all_gather | solution.py:246
  587.9 8.0 fusion.29
  595.9 4.5 all-gather.1
  600.4 2.0 convolution_add_fusion.2
  602.5 2.4 fusion.28
  604.9 4.8 all-gather
  609.7 116.3 %all-gather.16.cloned.1.call-done = bf16[1280,5120]{1,0:T(8,128)(2,1)} async-done(((bf16[80,5120]{1,0:T(8,128)(2,1)}), bf16[1280,5120]{1,0:T(8,128)(2,1)}) %all-gather.16.cloned.1.call-update) | async-done | bytes 13107216 | tf_op jit(solution)/shard_map/all_gather | solution.py:250
  726.0 6.7 fusion.167
  732.7 5.4 fusion.135
  738.2 1.8 fusion.171
  740.0 3.3 fusion.137
  743.3 16.1 fusion.9
  759.3 17.9 %multiply_reduce_fusion.3 = (f32[384]{0:T(512)S(1)}, f32[384]{0:T(512)S(1)}, f32[384,5120]{1,0:T(8,128)}) fusion(f32[5120]{0:T(1024)S(1)} %convert_element_type.349, f32[384,5120]{1,0:T(8,128)} %fusion.9, f32[5120]{0:T(1024)S(1)} %convert_element_type.348, f32[384,5120]{1,0:T(8,128)S(1)} %fusion.137, bf16[640,5120]{1,0:T(8,128)(2,1)} %collective-permute-done.3, ...), kind=kOutput, calls=%fused_computation.33 | convolution fusion | flops 5119671296 | bytes 37727232 | tf_op jit(solution)/shard_map/dot_general | solution.py:193
  778.6 12.4 convert_reduce_fusion.1
  791.0 12.3 fusion.52
  803.3 16.7 fusion.2
  820.0 17.6 %copy.89 = bf16[1280,5120]{1,0:T(8,128)(2,1)} copy(bf16[1280,5120]{0,1:T(8,128)(2,1)} %fusion.2) | data formatting | bytes 26214400
  840.2 3.4 fusion.136
  844.8 14.2 convolution_convert_fusion.5
  859.0 14.0 convolution_convert_fusion.4
  873.0 8.1 all-reduce.15
  886.0 10.5 convert_reduce_fusion.3
  896.5 10.6 multiply_reduce_fusion.7
  907.1 9.8 convert_reduce_fusion.2
  917.0 10.3 multiply_reduce_fusion.6
  929.6 2.7 fusion.13
  934.2 3.0 convolution_convert_fusion.3
  937.2 1.9 copy.70
  939.1 3.0 convolution_convert_fusion.2
  946.0 2.2 convolution_bitcast_fusion.5
  948.2 3.2 convolution_bitcast_fusion.4
  951.4 2.4 fusion.133
  953.8 3.1 convolution_bitcast_fusion.2
  956.9 3.1 convolution_bitcast_fusion.1
  962.7 8.3 fusion.116
  971.0 11.1 add_convert_fusion.4
  983.3 12.8 fusion.189
  996.0 15.6 add_convert_fusion.3
  1012.8 12.7 fusion.148
  1025.5 16.3 add_convert_fusion.2
  1042.4 13.9 fusion.169
  1056.3 19.7 %add_convert_fusion.1 = bf16[1280,5120]{1,0:T(8,128)(2,1)} fusion(f32[1280,5120]{1,0:T(8,128)} %fusion.169, f32[2,5120]{1,0:T(2,128)S(1)} %fusion.134, bf16[2,1,1280]{2,1,0:T(2,128)(2,1)S(1)} %copy-done.69), kind=kOutput, calls=%fused_computation.3 | convolution fusion | flops 170393600 | bytes 39367680 | tf_op jit(solution)/shard_map/dot_general | solution.py:209
  1077.4 2.3 copy.90
  1079.8 83.0 %reduce-scatter.9.cloned.1.call-done = bf16[80,3840]{1,0:T(8,128)(2,1)} async-done(((bf16[1280,3840]{1,0:T(8,128)(2,1)}), bf16[80,3840]{1,0:T(8,128)(2,1)}) %reduce-scatter.9.cloned.1.call-update) | async-done | bytes 614416 | tf_op jit(solution)/shard_map/reduce_scatter | solution.py:287
  1162.8 142.3 %reduce-scatter.13.cloned.1.call-done = bf16[80,5120]{1,0:T(8,128)(2,1)} async-done(((bf16[1280,5120]{1,0:T(8,128)(2,1)}), bf16[80,5120]{1,0:T(8,128)(2,1)}) %reduce-scatter.13.cloned.1.call-update) | async-done | bytes 819216 | tf_op jit(solution)/shard_map/reduce_scatter | solution.py:293
  1305.1 142.0 %reduce-scatter.15.cloned.1.call-done = bf16[320,1280]{1,0:T(8,128)(2,1)} async-done(((bf16[5120,1280]{1,0:T(8,128)(2,1)}), bf16[320,1280]{1,0:T(8,128)(2,1)}) %reduce-scatter.15.cloned.1.call-update) | async-done | bytes 819216 | tf_op jit(solution)/shard_map/reduce_scatter | solution.py:296
  1447.2 141.6 %reduce-scatter.17.cloned.1.call-done = bf16[80,5120]{1,0:T(8,128)(2,1)} async-done(((bf16[1280,5120]{1,0:T(8,128)(2,1)}), bf16[80,5120]{1,0:T(8,128)(2,1)}) %reduce-scatter.17.cloned.1.call-update) | async-done | bytes 819216 | tf_op jit(solution)/shard_map/reduce_scatter | solution.py:308
  1588.8 7.2 fusion.198
  1596.1 8.4 fusion.81
  1604.6 59.7 %all-reduce.12 = (bf16[1280]{0:T(1024)(128)(2,1)S(1)}, bf16[1280]{0:T(1024)(128)(2,1)S(1)}, bf16[5120]{0:T(1024)(128)(2,1)S(1)}, bf16[5120]{0:T(1024)(128)(2,1)S(1)}, bf16[5120]{0:T(1024)(128)(2,1)S(1)}) all-reduce(bf16[1280]{0:T(1024)(128)(2,1)S(1)} %add_convert_fusion.9, ...), channel_id=8, replica_groups=mesh['dp'=16,'query'=2] {'dp'}, use_global_device_ids=true, to_apply=%region_36.37.clone | all-reduce | flops 17920 | bytes 71680
  1664.7 5.0 all-reduce.14
  1676.1 33.7 %all-reduce.19.cloned.1.call-done = (bf16[80,5120]{0,1:T(8,128)(2,1)}, bf16[80,3840]{1,0:T(8,128)(2,1)}, bf16[80,1280]{1,0:T(8,128)(2,1)}, bf16[80,5120]{1,0:T(8...) async-done(((bf16[80,5120]{0,1:T(8,128)(2,1)}, bf16[80,3840]{1,0:T(8,128)(2,1)}, bf16[80,1280]{1,0:T(8,128)(2,1)}, bf16[80,5120]{1,0:T(8,128)(2,1)}, ...) | async-done | bytes 4096016 | tf_op jit(solution)/shard_map/psum | solution.py:330
  1709.8 2.6 convert_element_type.387
  (351 shorter events, 54.7 us)
Async XLA Ops:
  7.2 242.0 %all-gather.8.cloned.1.call-start = ((), (), s32[]{:S(2)}) async-start(), calls=%async_computation.6 | async-start | bytes 10444800 | tf_op jit(solution)/shard_map/all_gather | solution.py:243
  7.9 256.7 %all-gather.10.cloned.1.call-start = ((), (), s32[]{:S(2)}) async-start(), calls=%async_computation.7 | async-start | bytes 3481600 | tf_op jit(solution)/shard_map/all_gather | solution.py:244
  8.7 435.6 %all-gather.12.cloned.1.call-start = ((), (), s32[]{:S(2)}) async-start(), calls=%async_computation.8 | async-start | bytes 13926400 | tf_op jit(solution)/shard_map/all_gather | solution.py:245
  9.4 578.5 %all-gather.14.cloned.1.call-start = ((), (), s32[]{:S(2)}) async-start(), calls=%async_computation.9 | async-start | bytes 13926400 | tf_op jit(solution)/shard_map/all_gather | solution.py:246
  10.0 716.0 %all-gather.16.cloned.1.call-start = ((), (), s32[]{:S(2)}) async-start(), calls=%async_computation.10 | async-start | bytes 13926400 | tf_op jit(solution)/shard_map/all_gather | solution.py:250
  10.6 1066.9 %reduce-scatter.19.cloned.1.call-start = ((), (), s32[]{:S(2)}) async-start(), calls=%async_computation.16 | async-start | bytes 13926400
  10.6 2.6 collective-permute-start
  15.0 52.5 %collective-permute-start.1 = (bf16[160,5120]{1,0:T(8,128)(2,1)S(1)}, bf16[160,5120]{1,0:T(8,128)(2,1)}, u32[]{:S(2)}, u32[]{:S(2)}) collective-permute-start(bf16[160,5120]{1,0:T(8,128)(2,1)S(1)} %maximum_select_fusion.5), channel_id=1, source_target_pairs={{0,4},{2,6},{4,0},{6,2},{8,12},{10,14},{12,8},{14,10},{16,20},{18,... | collective-permute-start | bytes 4915208 | tf_op jit(solution)/shard_map/ppermute | solution.py:23
  17.9 54.7 %copy-start.96 = (u32[32]{0:T(128)S(1)}, u32[32]{0:T(128)}, u32[]{:S(2)}) copy-start(u32[32]{0:T(128)} %constant.116) | copy-start | bytes 388
  18.0 56.6 %copy-start.98 = (bf16[320]{0:T(512)(128)(2,1)S(1)}, bf16[320]{0:T(512)(128)(2,1)}, u32[]{:S(2)}) copy-start(bf16[320]{0:T(512)(128)(2,1)} %param.33) | copy-start | bytes 1924
  18.0 56.9 %copy-start.99 = (bf16[320]{0:T(512)(128)(2,1)S(1)}, bf16[320]{0:T(512)(128)(2,1)}, u32[]{:S(2)}) copy-start(bf16[320]{0:T(512)(128)(2,1)} %param.29) | copy-start | bytes 1924
  18.0 57.2 %copy-start.100 = (bf16[320]{0:T(512)(128)(2,1)S(1)}, bf16[320]{0:T(512)(128)(2,1)}, u32[]{:S(2)}) copy-start(bf16[320]{0:T(512)(128)(2,1)} %param.32) | copy-start | bytes 1924
  18.0 57.4 %copy-start.101 = (bf16[80]{0:T(256)(128)(2,1)S(1)}, bf16[80]{0:T(256)(128)(2,1)}, u32[]{:S(2)}) copy-start(bf16[80]{0:T(256)(128)(2,1)} %param.27) | copy-start | bytes 484
  18.0 57.6 %copy-start.102 = (bf16[80]{0:T(256)(128)(2,1)S(1)}, bf16[80]{0:T(256)(128)(2,1)}, u32[]{:S(2)}) copy-start(bf16[80]{0:T(256)(128)(2,1)} %param.28) | copy-start | bytes 484
  18.0 221.8 %copy-start.97 = (s32[1,2,1]{1,2,0:T(1,128)S(1)}, s32[1,2,1]{1,2,0:T(1,128)}, u32[]{:S(2)}) copy-start(s32[1,2,1]{1,2,0:T(1,128)} %param.37) | copy-start | bytes 28
  18.0 222.3 %copy-start.94 = (s32[2,1,384]{2,1,0:T(1,128)S(1)}, s32[2,1,384]{2,1,0:T(1,128)}, u32[]{:S(2)}) copy-start(s32[2,1,384]{2,1,0:T(1,128)} %param.35) | copy-start | bytes 9220
  18.0 222.3 %copy-start.95 = (s32[2,1,384]{2,1,0:T(1,128)S(1)}, s32[2,1,384]{2,1,0:T(1,128)}, u32[]{:S(2)}) copy-start(s32[2,1,384]{2,1,0:T(1,128)} %param.36) | copy-start | bytes 9220
  18.0 222.4 %copy-start.8 = (bf16[2,1,128,1280]{3,2,1,0:T(8,128)(2,1)S(1)}, bf16[2,1,128,1280]{3,2,1,0:T(8,128)(2,1)}, u32[]{:S(2)}) copy-start(bf16[2,1,128,1280]{3,2,1,0:T(8,128)(2,1)} %param.21) | copy-start | bytes 1966084
  71.2 169.8 %collective-permute-start.2 = (bf16[320,5120]{1,0:T(8,128)(2,1)}, bf16[320,5120]{1,0:T(8,128)(2,1)}, u32[]{:S(2)}, u32[]{:S(2)}) collective-permute-start(bf16[320,5120]{1,0:T(8,128)(2,1)} %maximum_select_fusion.2), channel_id=1, source_target_pairs={{0,8},{2,10},{4,12},{6,14},{8,0},{10,2},{12,4},{14,6},{16,24},{18,... | collective-permute-start | bytes 9830408 | tf_op jit(solution)/shard_map/ppermute | solution.py:23
  239.7 15.5 copy-start.51
  239.7 360.7 %copy-start.44 = (f32[1280]{0:T(1024)}, f32[1280]{0:T(1024)S(1)}, u32[]{:S(2)}) copy-start(f32[1280]{0:T(1024)S(1)} %convert_element_type.331) | copy-start | bytes 15364
  240.6 14.6 copy-start.83
  240.9 14.2 copy-start.90
  249.1 494.1 %collective-permute-start.3 = (bf16[640,5120]{1,0:T(8,128)(2,1)}, bf16[640,5120]{1,0:T(8,128)(2,1)}, u32[]{:S(2)}, u32[]{:S(2)}) collective-permute-start(bf16[640,5120]{1,0:T(8,128)(2,1)} %maximum_select_fusion.1), channel_id=1, source_target_pairs={{0,16},{2,18},{4,20},{6,22},{8,24},{10,26},{12,28},{14,30},{16,0},... | collective-permute-start | bytes 19660808 | tf_op jit(solution)/shard_map/ppermute | solution.py:23
  267.4 320.4 %copy-start.5 = (f32[128,1280]{1,0:T(8,128)}, f32[128,1280]{1,0:T(8,128)S(1)}, u32[]{:S(2)}) copy-start(f32[128,1280]{1,0:T(8,128)S(1)} %get-tuple-element.146) | copy-start | bytes 1966084
  267.5 176.8 %copy-start.81 = (f32[128]{0:T(128)}, f32[128]{0:T(128)S(1)}, u32[]{:S(2)}) copy-start(f32[128]{0:T(128)S(1)} %broadcast_multiply_fusion.8) | copy-start | bytes 1540
  271.4 331.1 %copy-start.10 = (f32[128,1280]{1,0:T(8,128)}, f32[128,1280]{1,0:T(8,128)S(1)}, u32[]{:S(2)}) copy-start(f32[128,1280]{1,0:T(8,128)S(1)} %get-tuple-element.150) | copy-start | bytes 1966084
  271.4 329.0 %copy-start.76 = (f32[128]{0:T(128)}, f32[128]{0:T(128)S(1)}, u32[]{:S(2)}) copy-start(f32[128]{0:T(128)S(1)} %broadcast_multiply_fusion.10) | copy-start | bytes 1540
  271.6 180.9 %copy-start.86 = (f32[128]{0:T(128)}, f32[128]{0:T(128)S(1)}, u32[]{:S(2)}) copy-start(f32[128]{0:T(128)S(1)} %add_rsqrt_fusion) | copy-start | bytes 1540
  271.7 328.8 %copy-start.79 = (f32[128]{0:T(128)}, f32[128]{0:T(128)S(1)}, u32[]{:S(2)}) copy-start(f32[128]{0:T(128)S(1)} %add_rsqrt_fusion.2) | copy-start | bytes 1540
  587.9 12.5 copy-start
  587.9 14.6 slice-start.4
  587.9 14.6 slice-start.5
  587.9 14.6 slice-start.6
  600.4 125.6 %copy-start.68 = (bf16[2,1,1280]{2,1,0:T(2,128)(2,1)}, bf16[2,1,1280]{2,1,0:T(2,128)(2,1)S(1)}, u32[]{:S(2)}) copy-start(bf16[2,1,1280]{2,1,0:T(2,128)(2,1)S(1)} %all-gather.1) | copy-start | bytes 15364
  604.9 127.8 %copy-start.55 = (bf16[128,1280]{1,0:T(8,128)(2,1)}, bf16[128,1280]{1,0:T(8,128)(2,1)S(1)}, u32[]{:S(2)}) copy-start(bf16[128,1280]{1,0:T(8,128)(2,1)S(1)} %fusion.28) | copy-start | bytes 983044
  609.7 128.4 %copy-start.70 = (bf16[2,1,1280]{2,1,0:T(2,128)(2,1)}, bf16[2,1,1280]{2,1,0:T(2,128)(2,1)S(1)}, u32[]{:S(2)}) copy-start(bf16[2,1,1280]{2,1,0:T(2,128)(2,1)S(1)} %all-gather) | copy-start | bytes 15364
  726.0 12.1 slice-start
  726.0 12.1 slice-start.1
  726.0 12.1 slice-start.2
  759.3 19.2 %copy-start.24 = (f32[384,5120]{1,0:T(8,128)S(1)}, f32[384,5120]{1,0:T(8,128)}, u32[]{:S(2)}) copy-start(f32[384,5120]{1,0:T(8,128)} %fusion.9) | copy-start | bytes 23592964
  791.0 12.3 copy-start.4
  837.6 242.2 %reduce-scatter.11.cloned.1.call-start = ((), (), s32[]{:S(2)}) async-start(), calls=%async_computation.12 | async-start | bytes 3481600 | tf_op jit(solution)/shard_map/reduce_scatter | solution.py:290
  859.0 27.0 %copy-start.19 = (f32[128,5120]{1,0:T(8,128)S(1)}, f32[128,5120]{1,0:T(8,128)}, u32[]{:S(2)}) copy-start(f32[128,5120]{1,0:T(8,128)} %copy-done.18) | copy-start | bytes 7864324
  883.1 45.3 %copy-start.25 = (f32[128,1280]{1,0:T(8,128)}, f32[128,1280]{1,0:T(8,128)S(1)}, u32[]{:S(2)}) copy-start(f32[128,1280]{1,0:T(8,128)S(1)} %scatter-add.9) | copy-start | bytes 1966084
  886.0 10.5 copy-start.11
  886.0 10.5 copy-start.45
  886.0 10.5 copy-start.77
  886.0 10.5 copy-start.80
  896.5 10.6 copy-start.29
  896.5 10.6 copy-start.13
  917.0 10.4 copy-start.30
  932.3 230.5 %reduce-scatter.9.cloned.1.call-start = ((), (), s32[]{:S(2)}) async-start(), calls=%async_computation.11 | async-start | bytes 10444800 | tf_op jit(solution)/shard_map/reduce_scatter | solution.py:287
  982.2 13.8 copy-start.7
  982.2 322.9 %reduce-scatter.13.cloned.1.call-start = ((), (), s32[]{:S(2)}) async-start(), calls=%async_computation.13 | async-start | bytes 13926400 | tf_op jit(solution)/shard_map/reduce_scatter | solution.py:293
  1011.7 13.7 copy-start.26
  1011.7 435.5 %reduce-scatter.15.cloned.1.call-start = ((), (), s32[]{:S(2)}) async-start(), calls=%async_computation.14 | async-start | bytes 13926400 | tf_op jit(solution)/shard_map/reduce_scatter | solution.py:296
  1041.8 14.5 copy-start.69
  1041.8 547.0 %reduce-scatter.17.cloned.1.call-start = ((), (), s32[]{:S(2)}) async-start(), calls=%async_computation.15 | async-start | bytes 13926400 | tf_op jit(solution)/shard_map/reduce_scatter | solution.py:308
  1076.1 633.8 %all-reduce.19.cloned.1.call-start = ((), (), s32[]{:S(2)}) async-start(), calls=%async_computation.17 | async-start | bytes 9175040 | tf_op jit(solution)/shard_map/psum | solution.py:330
  1596.1 76.4 %copy-start.54 = (bf16[128,1280]{1,0:T(8,128)(2,1)S(1)}, bf16[128,1280]{1,0:T(8,128)(2,1)}, u32[]{:S(2)}) copy-start(bf16[128,1280]{1,0:T(8,128)(2,1)} %copy-done.53) | copy-start | bytes 983044
  1596.1 76.4 %copy-start.56 = (bf16[128,1280]{1,0:T(8,128)(2,1)S(1)}, bf16[128,1280]{1,0:T(8,128)(2,1)}, u32[]{:S(2)}) copy-start(bf16[128,1280]{1,0:T(8,128)(2,1)} %copy-done.55) | copy-start | bytes 983044
  1596.1 77.3 %copy-start.21 = (f32[128,1280]{1,0:T(8,128)S(1)}, f32[128,1280]{1,0:T(8,128)}, u32[]{:S(2)}) copy-start(f32[128,1280]{1,0:T(8,128)} %copy-done.20) | copy-start | bytes 1966084
  1596.1 77.3 %copy-start.23 = (f32[128,1280]{1,0:T(8,128)S(1)}, f32[128,1280]{1,0:T(8,128)}, u32[]{:S(2)}) copy-start(f32[128,1280]{1,0:T(8,128)} %copy-done.22) | copy-start | bytes 1966084
  (64 other events, 272.0 us)
Sparse Core Ops, SparseCore 0:
  10.3 104.4 all-gather.7
  117.1 60.6 all-gather.9
  180.1 264.1 all-gather.11
  446.4 141.4 all-gather.13
  590.0 135.9 all-gather.15
  837.7 137.3 reduce-scatter.18
  979.4 65.8 reduce-scatter.10
  1049.5 113.2 reduce-scatter.8
  1166.9 138.1 reduce-scatter.12
  1309.6 137.5 reduce-scatter.14
  1451.3 137.4 reduce-scatter.16
  1592.5 117.3 all-reduce.18
